TPU v7x, 128 devices: a whole 4x4x4 slice. The times are simulated.
128 devices in a mesh: coarse: 8 (over y, z_lo), fine: 16 (over x, z_hi, core).
Axes of the slice: x: 4, y: 4, z: 4 (z_hi: 2, z_lo: 2; z = z_hi * 2 + z_lo), core: 2. Of those that a mesh axis runs over, the one named last changes fastest.
Arguments:
- field_in: float32 [512, 2, 256, 256], P(('coarse', 'fine')), may hold values from -6 to 6
- phases: float32 [512, 1024], P(('coarse', 'fine')), may hold values from -3.140625 to 3.140625
- energy: float32 [512, 1024], P(('coarse', 'fine')), may hold values from -4 to 4
- cell_index: int32 [512, 2, 1024], P(('coarse', 'fine')), may hold values from 0 to 255
- offsets: float32 [512, 2, 1024], P(('coarse', 'fine')), may hold values from -0.5 to 0.5
- slip_plan: int32 [4], replicated, may hold values from 1 to 2, as said below
- bragg_response: float32 [2, 512], replicated, may hold values from -1 to 1
Outputs:
- field_out: float32 [512, 2, 256, 256], P(('coarse', 'fine'))
- particles: float32 [512, 2, 1024], P(('coarse', 'fine'))
Inputs may be any that keep to these rules, and one draw needn't show every extreme that they name: `slip_plan`: each undulator step slips the field by 1 or 2 slices; at least one step slips by 1 and at least one by 2.
All inputs are finite; a program needn't handle non-finite values.
Results may differ from a plain program's by a relative error of at most 0.0065.
Values sent between devices are 32-bit elements; how exact they have to be, the bound alone decides.
A program may use at most 192 MiB of HBM per device.

v0:
```python
import functools
import itertools

import jax
import jax.numpy as jnp
import numpy as np
from jax import lax
from jax.experimental import pallas as pl
from jax.experimental.pallas import tpu as pltpu
from jax.sharding import PartitionSpec as P

W = 256
HALF = 128
P_SIZE = 1024
STEPS = 4
NS = 512
CHAINS = 4
COARSE = 8
FINE = 16
DEVICES = COARSE * FINE
REACH = 10
GAIN = 0.25 * W * W / P_SIZE
SPREAD = 20.0
MESH = pl.DeviceIdType.MESH
f32, bf16 = jnp.float32, jnp.bfloat16


def halves(matrix):
    high = matrix.astype(np.float32).astype(bf16)
    low = (matrix - high.astype(np.float64)).astype(np.float32).astype(bf16)
    return high, low


def diffraction_tables():
    k = np.arange(W)
    signed = np.where(k < W // 2, k, k - W)
    h = np.exp(-1j * SPREAD * (2.0 * np.pi * signed / W) ** 2)
    q = np.fft.ifft(h)
    full = q[(k[:, None] - k[None, :]) % W]
    a, b = full[:HALF, :HALF], full[:HALF, HALF:]
    right, left = [], []
    for part in (0.5 * (a + b), 0.5 * (a - b)):
        t = part.T
        hi, lo = halves(np.block([[t.real, t.imag], [-t.imag, t.real]]))
        right.append(np.concatenate([hi, lo, hi], axis=0))
        hi, lo = halves(np.block([[part.real, -part.imag], [part.imag, part.real]]))
        left.append(np.concatenate([hi, hi, lo], axis=1))
    return np.stack(right), np.stack(left)


def time_tables():
    m = np.arange(NS // 2)
    t = np.arange(NS // 2)
    tables = []
    for parity in (0, 1):
        angle = 2.0 * np.pi * ((2 * m[:, None] + parity) * t[None, :] % NS) / NS
        c, s = np.cos(angle), np.sin(angle)
        full = np.stack([np.stack([c, s], 1), np.stack([-s, c], 1)], 0)
        full = full.reshape(2, NS // 2, 2, NS // 8, CHAINS).transpose(0, 1, 3, 2, 4).reshape(NS, NS)
        tables.append(np.stack(halves(full)))
    return np.stack(tables)


def place(n):
    n = lax.rem(n + 2 * DEVICES, DEVICES)
    return (n // FINE, lax.rem(n, FINE))


def my_index():
    return lax.axis_index("coarse") * FINE + lax.axis_index("fine")


def sincos(x):
    turns = jnp.round(x * (2.0 / np.pi))
    r = x - turns * 1.5703125
    r = r - turns * 4.837512969970703125e-4
    r = r - turns * 7.54978995489188216e-8
    z = r * r
    sine = r + r * z * (-1.6666654611e-1 + z * (8.3321608736e-3 + z * -1.9515295891e-4))
    cosine = 1.0 - 0.5 * z + z * z * (4.166664568298827e-2 + z * (-1.388731625493765e-3 + z * 2.443315711809948e-5))
    quadrant = turns.astype(jnp.int32) & 3
    odd = (quadrant & 1) == 1
    s = jnp.where(odd, cosine, sine)
    c = jnp.where(odd, sine, cosine)
    s = jnp.where(quadrant >= 2, -s, s)
    c = jnp.where((quadrant == 1) | (quadrant == 2), -c, c)
    return s, c


def spline_rows(table, r, cells, shifts):
    near = shifts
    left = (0.5 * (0.5 - near) * (0.5 - near)).astype(bf16).astype(f32)
    middle = (0.75 - near * near).astype(bf16).astype(f32)
    right = (0.5 * (0.5 + near) * (0.5 + near)).astype(bf16).astype(f32)
    before = (cells - 1) & (W - 1)
    after = (cells + 1) & (W - 1)
    step = 32
    for row in range(0, W, step):
        grid = lax.broadcasted_iota(jnp.int32, (step, P_SIZE), 0) + row
        value = jnp.where(grid == before, left, 0.0)
        value = jnp.where(grid == cells, middle, value)
        value = jnp.where(grid == after, right, value)
        table[r, row : row + step, :] = value.astype(bf16)


def steps_kernel(
    slip, field_in, phases, energy, cells, shifts, mright, mleft, out, ends,
    field, tx, ty, gcells, gshifts, state, arrived, dep, cur, lhs, rhs, rounded,
    load_sem, gs, gr, ps, pr,
):
    me = my_index()
    barrier = pltpu.get_barrier_semaphore()
    for step in (-2, -1, 1, 2):
        pl.semaphore_signal(barrier, inc=1, device_id=place(me + step), device_id_type=MESH)
    load = pltpu.make_async_copy(field_in, field, load_sem)
    load.start()
    gcells[0:CHAINS] = cells[...]
    gshifts[0:CHAINS] = shifts[...]
    pl.semaphore_wait(barrier, 4)
    sends = []
    for n, (src, dst) in enumerate(((cells, gcells), (shifts, gshifts))):
        sends.append(pltpu.make_async_remote_copy(
            src, dst.at[pl.ds(4, 4)], gs.at[n], gr.at[n], device_id=place(me - 1), device_id_type=MESH))
        sends.append(pltpu.make_async_remote_copy(
            src.at[pl.ds(0, 2)], dst.at[pl.ds(8, 2)], gs.at[n + 2], gr.at[n + 2], device_id=place(me - 2), device_id_type=MESH))
    for copy in sends:
        copy.start()

    def build(r, carry):
        spline_rows(tx, r, gcells[r, 0:1, :], gshifts[r, 0:1, :])
        spline_rows(ty, r, gcells[r, 1:2, :], gshifts[r, 1:2, :])
        return carry

    lax.fori_loop(0, CHAINS, build, 0)
    for copy in sends:
        copy.wait()
    lax.fori_loop(CHAINS, REACH, build, 0)
    load.wait()

    def pair(u, base, theta, eta):
        met = slip[STEPS + u]
        sine, cosine = sincos(theta)
        for k in range(2):
            r = base + k + met
            c, s = cosine[k : k + 1], -sine[k : k + 1]
            for row in range(0, W, 32):
                weights = tx[r, row : row + 32, :].astype(f32)
                dep[k, row : row + 32, :] = (weights * c).astype(bf16)
                dep[k, W + row : W + row + 32, :] = (weights * s).astype(bf16)
            cur[k] = lax.dot_general(dep[k], ty[r], (((1,), (1,)), ((), ())), preferred_element_type=f32)
        for k in range(2):
            chain = base + k
            at = me * CHAINS + chain
            fresh = (at + met >= NS) & (at + slip[2 * STEPS + u] < NS)
            keep = jnp.where(fresh, 0.0, 1.0)
            for c in range(2):
                for row in range(0, HALF, 32):
                    top = field[chain, c, row : row + 32, :] * keep + GAIN * cur[k, c * W + row : c * W + row + 32, :]
                    low = row + HALF
                    bottom = field[chain, c, low : low + 32, :] * keep + GAIN * cur[k, c * W + low : c * W + low + 32, :]
                    for sx, v in enumerate((top + bottom, top - bottom)):
                        a, b = v[:, :HALF], v[:, HALF:]
                        rows = slice(sx * HALF + row, sx * HALF + row + 32)
                        for sy, g in enumerate((a + b, a - b)):
                            hi = g.astype(bf16)
                            lo = (g - hi.astype(f32)).astype(bf16)
                            lhs[k, sy, rows, c * HALF : c * HALF + HALF] = hi
                            lhs[k, sy, rows, W + c * HALF : W + c * HALF + HALF] = hi
                            lhs[k, sy, rows, 2 * W + c * HALF : 2 * W + c * HALF + HALF] = lo
            for sy in range(2):
                mid = jnp.dot(lhs[k, sy], mright[sy], preferred_element_type=f32)
                for sx in range(2):
                    for c in range(2):
                        g = mid[sx * HALF : sx * HALF + HALF, c * HALF : c * HALF + HALF]
                        hi = g.astype(bf16)
                        lo = (g - hi.astype(f32)).astype(bf16)
                        cols = slice(sy * HALF, sy * HALF + HALF)
                        rhs[k, sx, c * HALF : c * HALF + HALF, cols] = hi
                        rhs[k, sx, W + c * HALF : W + c * HALF + HALF, cols] = lo
                        rhs[k, sx, 2 * W + c * HALF : 2 * W + c * HALF + HALF, cols] = hi
        for k in range(2):
            chain = base + k
            za = jnp.dot(mleft[0], rhs[k, 0], preferred_element_type=f32)
            zb = jnp.dot(mleft[1], rhs[k, 1], preferred_element_type=f32)
            for c in range(2):
                p, n = za[c * HALF : c * HALF + HALF], zb[c * HALF : c * HALF + HALF]
                for hx, v in enumerate((p + n, p - n)):
                    a, b = v[:, :HALF], v[:, HALF:]
                    for hy, g in enumerate((a + b, a - b)):
                        rows = slice(hx * HALF, hx * HALF + HALF)
                        cols = slice(hy * HALF, hy * HALF + HALF)
                        field[chain, c, rows, cols] = g
                        rounded[k, c * W + hx * HALF : c * W + hx * HALF + HALF, cols] = g.astype(bf16)
        sampled = []
        for k in range(2):
            r = base + k + met
            pieces = []
            for q in range(0, P_SIZE, 256):
                picked = jnp.dot(rounded[k], ty[r, :, q : q + 256], preferred_element_type=f32)
                weights = tx[r, :, q : q + 256].astype(f32)
                pieces.append([jnp.sum(picked[c * W : c * W + W] * weights, axis=0, keepdims=True) for c in range(2)])
            sampled.append([jnp.concatenate([piece[c] for piece in pieces], axis=1) for c in range(2)])
        first = jnp.concatenate([sampled[0][0], sampled[1][0]], axis=0)
        second = jnp.concatenate([sampled[0][1], sampled[1][1]], axis=0)
        eta = eta - 0.5 * (first * cosine - second * sine)
        return theta + eta, eta

    def store(u, base, theta, eta):
        state[u, 0, base : base + 2, :] = theta
        state[u, 1, base : base + 2, :] = eta

    def exchange(u):
        return [
            pltpu.make_async_remote_copy(
                state.at[u, n, pl.ds(0, 2)], arrived.at[u, n], ps.at[u, n], pr.at[u, n],
                device_id=place(me - 1), device_id_type=MESH)
            for n in range(2)
        ]

    theta, eta = phases[0:2], energy[0:2]
    moving = None
    for u in range(STEPS):
        if u:
            one = slip[u - 1] == 1
            theta, eta = (jnp.where(one, state[u - 1, n, 1:3, :], state[u - 1, n, 2:4, :]) for n in range(2))
        theta, eta = pair(u, 0, theta, eta)
        store(u, 0, theta, eta)
        if u:
            for copy in moving:
                copy.wait()
            theta, eta = (
                jnp.where(
                    one,
                    jnp.concatenate([state[u - 1, n, 3:4, :], arrived[u - 1, n, 0:1, :]], axis=0),
                    arrived[u - 1, n],
                )
                for n in range(2)
            )
        else:
            theta, eta = phases[2:4], energy[2:4]
        if u < STEPS - 1:
            moving = exchange(u)
            for copy in moving:
                copy.start()
        theta, eta = pair(u, 2, theta, eta)
        store(u, 2, theta, eta)
    for chain in range(CHAINS):
        at = me * CHAINS + chain
        gone = (at + slip[3 * STEPS] >= NS) & (at + slip[2 * STEPS - 1] < NS)
        keep = jnp.where(gone, 0.0, 1.0)
        for c in range(2):
            for hx in range(2):
                for hy in range(2):
                    out[2 * hx + hy, pl.ds(c * CHAINS + chain, HALF, stride=8), :] = (
                        field[chain, c, hx * HALF : hx * HALF + HALF, hy * HALF : hy * HALF + HALF] * keep
                    )
    ends[...] = state[STEPS - 1]


def far_first():
    offsets = [o for o in itertools.product(range(4), range(4), range(4), range(2)) if any(o)]
    mixed = np.random.RandomState(1).permutation(len(offsets))
    offsets = [offsets[i] for i in mixed]
    return sorted(offsets, key=lambda o: -sum(min(v, 4 - v) for v in o[:3]))


def partners():
    coarse, fine = lax.axis_index("coarse"), lax.axis_index("fine")
    x, y = fine // 4, coarse // 2
    z, core = (lax.rem(fine, 4) // 2) * 2 + lax.rem(coarse, 2), lax.rem(fine, 2)
    out = []
    for dx, dy, dz, dk in far_first():
        px, py, pz, pk = lax.rem(x + dx, 4), lax.rem(y + dy, 4), lax.rem(z + dz, 4), lax.rem(core + dk, 2)
        out.append((py * 2 + lax.rem(pz, 2), px * 4 + (pz // 2) * 2 + pk))
    return out


PARTS = 2
TILES = 4 // PARTS
WIDTH = TILES * HALF


def filter_kernel(
    slip, sent, ends, columns, tables, back, particles,
    table, got, result, scaled, conv, operand, homes,
    table_sem, own_sem, s1, r1, s2, r2, hs, hr,
):
    me = my_index()
    others = partners()
    barrier = pltpu.get_barrier_semaphore()
    for there in others:
        pl.semaphore_signal(barrier, inc=1, device_id=there, device_id_type=MESH)
    load = pltpu.make_async_copy(tables, table, table_sem)
    load.start()
    pl.semaphore_wait(barrier, DEVICES - 1)

    def spread(src, dst, q, ss, rs):
        tiles = pl.ds(q * TILES, TILES)
        for there in others:
            pltpu.make_async_remote_copy(
                src.at[tiles, there[0] * FINE + there[1]], dst.at[tiles, me], ss.at[q], rs.at[q],
                device_id=there, device_id_type=MESH).start()

    def settle(ref, q, sem):
        view = ref.at[pl.ds(q * TILES, TILES), pl.ds(0, DEVICES - 1)]
        pltpu.make_async_copy(view, view, sem.at[q]).wait()

    for q in range(PARTS):
        spread(sent, got, q, s1, r1)
    own = pltpu.make_async_copy(sent.at[:, me], got.at[:, me], own_sem.at[0])
    own.start()
    homing = [
        pltpu.make_async_remote_copy(
            ends, homes.at[n], hs.at[n], hr.at[n], device_id=place(me + n + 1), device_id_type=MESH)
        for n in range(2)
    ]
    for copy in homing:
        copy.start()
    load.wait()
    quarter = NS // 2
    for parity in range(2):
        re, im = columns[:, 2 * parity : 2 * parity + 1], columns[:, 2 * parity + 1 : 2 * parity + 2]
        for row in range(0, quarter, 64):
            rows, below = slice(row, row + 64), slice(quarter + row, quarter + row + 64)
            wr = table[parity, 0, rows, :].astype(f32) + table[parity, 1, rows, :].astype(f32)
            wi = table[parity, 0, below, :].astype(f32) + table[parity, 1, below, :].astype(f32)
            for start, g in (
                (row, re[rows] * wr - im[rows] * wi),
                (quarter + row, im[rows] * wr + re[rows] * wi),
            ):
                hi = g.astype(bf16)
                scaled[0, start : start + 64, :] = hi
                scaled[1, start : start + 64, :] = (g - hi.astype(f32)).astype(bf16)
        dims = (((0,), (0,)), ((), ()))
        kernel = (
            lax.dot_general(table[parity, 0], scaled[0], dims, preferred_element_type=f32)
            + lax.dot_general(table[parity, 0], scaled[1], dims, preferred_element_type=f32)
            + lax.dot_general(table[parity, 1], scaled[0], dims, preferred_element_type=f32)
        )
        hi = kernel.astype(bf16)
        conv[parity, :, 0:NS] = hi
        conv[parity, :, NS : 2 * NS] = hi
        conv[parity, :, 2 * NS : 3 * NS] = (kernel - hi.astype(f32)).astype(bf16)
    own.wait()
    mid = DEVICES // 2
    for q in range(PARTS):
        settle(got, q, r1)
        for tile in range(TILES):
            lanes = slice(tile * HALF, tile * HALF + HALF)
            for block in range(0, mid, 8):
                a = got[q * TILES + tile, block : block + 8].reshape(64, HALF)
                b = got[q * TILES + tile, mid + block : mid + block + 8].reshape(64, HALF)
                for parity, g in enumerate((a + b, a - b)):
                    hi = g.astype(bf16)
                    rows = block * 8
                    operand[parity, rows : rows + 64, lanes] = hi
                    operand[parity, NS + rows : NS + rows + 64, lanes] = (g - hi.astype(f32)).astype(bf16)
                    operand[parity, 2 * NS + rows : 2 * NS + rows + 64, lanes] = hi
        for block in range(0, NS, 256):
            even = jnp.dot(conv[0, block : block + 256, :], operand[0], preferred_element_type=f32)
            odd = jnp.dot(conv[1, block : block + 256, :], operand[1], preferred_element_type=f32)
            for tile in range(TILES):
                lanes = slice(tile * HALF, tile * HALF + HALF)
                a, b = even[:, lanes], odd[:, lanes]
                result[q * TILES + tile, block // 8 : block // 8 + 32] = (a + b).reshape(32, 8, HALF)
                result[q * TILES + tile, mid + block // 8 : mid + block // 8 + 32] = (a - b).reshape(32, 8, HALF)
        spread(result, back, q, s2, r2)
    own = pltpu.make_async_copy(result.at[:, me], back.at[:, me], own_sem.at[1])
    own.start()
    for copy in homing:
        copy.wait()
    met = slip[2 * STEPS - 1]
    for i in range(CHAINS):
        at = i - met
        for n in range(2):
            value = homes[1, n, pl.ds(jnp.clip(at + 8, 0, 3), 1), :]
            value = jnp.where(at >= -4, homes[0, n, pl.ds(jnp.clip(at + 4, 0, 3), 1), :], value)
            value = jnp.where(at >= 0, ends[n, pl.ds(jnp.clip(at, 0, 3), 1), :], value)
            particles[i, n : n + 1, :] = value
    own.wait()
    for q in range(PARTS):
        settle(got, q, s1)
        settle(got, q, s2)
        settle(got, q, r2)


def unblock_kernel(blocks, out):
    for chain in range(CHAINS):
        for c in range(2):
            for hx in range(2):
                for hy in range(2):
                    out[chain, c, hx, :, hy * HALF : hy * HALF + HALF] = blocks[
                        2 * hx + hy, pl.ds(c * CHAINS + chain, 32, stride=8), :
                    ]


def on_device(field_in, phases, energy, cell_index, offsets, slip_plan, bragg_response):
    slip_plan = slip_plan.astype(jnp.int32)
    met = jnp.concatenate([jnp.zeros((1,), jnp.int32), jnp.cumsum(slip_plan)])
    before = jnp.concatenate([jnp.zeros((1,), jnp.int32), met[: STEPS - 1]])
    slip = jnp.concatenate([slip_plan, met[:STEPS], before, met[STEPS:]])
    mright, mleft = diffraction_tables()
    vmem = pl.BlockSpec(memory_space=pltpu.VMEM)
    smem = pl.BlockSpec(memory_space=pltpu.SMEM)
    whole = pl.BlockSpec(memory_space=pl.ANY)
    dma = pltpu.SemaphoreType.DMA
    sent, ends = pl.pallas_call(
        steps_kernel,
        out_shape=(
            jax.ShapeDtypeStruct((4, DEVICES * 8, HALF), f32),
            jax.ShapeDtypeStruct((2, CHAINS, P_SIZE), f32),
        ),
        in_specs=[smem, whole] + [vmem] * 6,
        out_specs=(vmem, vmem),
        scratch_shapes=[
            pltpu.VMEM((CHAINS, 2, W, W), f32),
            pltpu.VMEM((REACH, W, P_SIZE), bf16),
            pltpu.VMEM((REACH, W, P_SIZE), bf16),
            pltpu.VMEM((REACH, 2, P_SIZE), jnp.int32),
            pltpu.VMEM((REACH, 2, P_SIZE), f32),
            pltpu.VMEM((STEPS, 2, CHAINS, P_SIZE), f32),
            pltpu.VMEM((STEPS, 2, 2, P_SIZE), f32),
            pltpu.VMEM((2, 2 * W, P_SIZE), bf16),
            pltpu.VMEM((2, 2 * W, W), f32),
            pltpu.VMEM((2, 2, W, 3 * W), bf16),
            pltpu.VMEM((2, 2, 3 * W, W), bf16),
            pltpu.VMEM((2, 2 * W, W), bf16),
            dma,
            dma((4,)),
            dma((4,)),
            dma((STEPS, 2)),
            dma((STEPS, 2)),
        ],
        compiler_params=pltpu.CompilerParams(
            collective_id=0, has_side_effects=True, vmem_limit_bytes=56 << 20
        ),
        name="steps",
    )(slip, field_in, phases, energy, cell_index, offsets, jnp.asarray(mright), jnp.asarray(mleft))

    frequency = jnp.arange(NS, dtype=jnp.int32)
    angle = (-2.0 * np.pi / NS) * (frequency * met[STEPS] % NS).astype(f32)
    turn_real, turn_quad = jnp.cos(angle) / NS, jnp.sin(angle) / NS
    real = bragg_response[0] * turn_real - bragg_response[1] * turn_quad
    quad = bragg_response[0] * turn_quad + bragg_response[1] * turn_real
    columns = jnp.stack([real.reshape(NS // 2, 2), quad.reshape(NS // 2, 2)], axis=2).reshape(NS // 2, 4)
    back, particles = pl.pallas_call(
        filter_kernel,
        out_shape=(
            jax.ShapeDtypeStruct((4, DEVICES, 8, HALF), f32),
            jax.ShapeDtypeStruct((CHAINS, 2, P_SIZE), f32),
        ),
        in_specs=[smem, whole, vmem, vmem, whole],
        out_specs=(whole, vmem),
        scratch_shapes=[
            pltpu.VMEM((2, 2, NS, NS), bf16),
            pltpu.VMEM((4, DEVICES, 8, HALF), f32),
            pltpu.VMEM((4, DEVICES, 8, HALF), f32),
            pltpu.VMEM((2, NS, NS), bf16),
            pltpu.VMEM((2, NS, 3 * NS), bf16),
            pltpu.VMEM((2, 3 * NS, WIDTH), bf16),
            pltpu.VMEM((2, 2, CHAINS, P_SIZE), f32),
            dma,
            dma((2,)),
            dma((PARTS,)),
            dma((PARTS,)),
            dma((PARTS,)),
            dma((PARTS,)),
            dma((2,)),
            dma((2,)),
        ],
        compiler_params=pltpu.CompilerParams(
            collective_id=1, has_side_effects=True, vmem_limit_bytes=40 << 20
        ),
        name="filter",
    )(slip, sent.reshape(4, DEVICES, 8, HALF), ends, columns, jnp.asarray(time_tables()))

    field_out = pl.pallas_call(
        unblock_kernel,
        grid=(4,),
        out_shape=jax.ShapeDtypeStruct((CHAINS, 2, 2, HALF, W), f32),
        in_specs=[pl.BlockSpec((4, 256, HALF), lambda i: (0, i, 0))],
        out_specs=pl.BlockSpec((CHAINS, 2, 2, 32, W), lambda i: (0, 0, 0, i, 0)),
        name="unblock",
    )(back.reshape(4, DEVICES * 8, HALF))
    return field_out.reshape(CHAINS, 2, W, W), particles


def solution(mesh):
    axes = ("coarse", "fine")
    in_specs = (
        P(axes, None, None, None),
        P(axes, None),
        P(axes, None),
        P(axes, None, None),
        P(axes, None, None),
        P(),
        P(),
    )
    out_specs = (P(axes, None, None, None), P(axes, None, None))
    return jax.shard_map(on_device, mesh=mesh, in_specs=in_specs, out_specs=out_specs, check_vma=False)
```

profile of v0, /device:TPU:35, one launch (start us, length us, event | category | flops | bytes accessed | tf_op | source)
XLA Modules:
  0.0 120.7 jit_solution(14253454104553605228)
XLA Ops:
  0.6 0.8 reduce-window.4
  1.5 0.6 slice.23
  2.0 0.1 pad_add_fusion
  2.1 1.9 %concatenate.7.slip = s32[13]{0:T(128)} concatenate(s32[4]{0:T(128)} %param.15, s32[4]{0:T(128)S(1)} %bitcast.14, s32[1]{0:T(128)} %constant.28.clone.1, s32[3]{0:T(128)S(1)} %bitcast.15, s32[1]{0:T(128)} %bitcast.2), dimensions={0} | concatenate | bytes 104 | tf_op jit(solution)/shard_map/concatenate | solution.py:401
  4.0 0.8 slice_reduce_fusion.1
  4.8 0.1 squeeze.11
  4.9 0.1 copy.21
  5.0 0.0 copy-start
  5.0 0.0 copy-start.4
  5.0 0.1 squeeze.13
  5.2 0.1 copy.22
  5.2 0.8 multiply_subtract_fusion
  6.1 0.1 copy.27.columns
  6.3 34.2 %steps.1 = (f32[4,1024,128]{2,1,0:T(8,128)}, f32[2,4,1024]{2,1,0:T(4,128)}) custom-call(s32[13]{0:T(128)} %concatenate.7.slip, f32[4,2,256,256]{3,2,1,0:T(8,128)} %field_in.1, f32[4,1024]{1,0:T(4,128)} %phases.1, f32[4,1024]{1,0:T(4,128)} %energy.1, s32[4,2,1024]{2,1,0:T(2,128)} %cells.1, f32[4,2,1024]{2,1,0:T(2,128)} %shifts.1, ...), custom_call_target="tpu_custom_call" | custom-call | tf_op jit(solution)/shard_map/steps/pallas_call | solution.py:407
  40.5 0.0 copy-done
  40.5 0.0 copy-done.4
  40.5 0.0 copy-start.1
  40.5 1.6 %copy-done.1 = f32[4,1024,128]{2,1,0:T(8,128)S(1)} copy-done((f32[4,1024,128]{2,1,0:T(8,128)S(1)}, f32[4,1024,128]{2,1,0:T(8,128)}, u32[]{:S(2)}) %copy-start.1) | copy-done | bytes 2097176
  42.1 0.0 copy-start.3
  42.1 0.8 copy-done.3
  42.8 72.0 %filter.1 = (f32[4,128,8,128]{3,2,1,0:T(8,128)S(1)}, f32[4,2,1024]{2,1,0:T(2,128)S(1)}) custom-call(s32[13]{0:T(128)S(1)} %copy-done.4, f32[4,128,8,128]{3,2,1,0:T(8,128)S(1)} %bitcast.11, f32[2,4,1024]{2,1,0:T(4,128)S(1)} %copy-done.3, f32[256,4]{1,0:T(8,128)S(1)} %copy.27.columns, bf16[2,2,512,512]{3,2,1,0:T(8,128)(2,1)S(1)} %copy-done), custom_call_target="tpu_custom_call" | custom-call | tf_op jit(solution)/shard_map/filter/pallas_call | solution.py:446
  114.8 0.0 copy-start.2
  114.8 1.3 %copy-done.2 = f32[4,128,8,128]{3,2,1,0:T(8,128)} copy-done((f32[4,128,8,128]{3,2,1,0:T(8,128)}, f32[4,128,8,128]{3,2,1,0:T(8,128)S(1)}, u32[]{:S(2)}) %copy-start.2) | copy-done | bytes 2097176
  116.2 3.9 %unblock.1 = f32[4,2,2,128,256]{4,3,2,1,0:T(8,128)} custom-call(f32[4,1024,128]{2,1,0:T(8,128)} %bitcast.12), custom_call_target="tpu_custom_call" | custom-call | tf_op jit(solution)/shard_map/unblock/pallas_call | solution.py:477
  120.1 0.6 copy.29
  (4 shorter events, 0.0 us)
Async XLA Ops:
  5.0 35.5 %copy-start = (bf16[2,2,512,512]{3,2,1,0:T(8,128)(2,1)S(1)}, bf16[2,2,512,512]{3,2,1,0:T(8,128)(2,1)}, u32[]{:S(2)}) copy-start(bf16[2,2,512,512]{3,2,1,0:T(8,128)(2,1)} %constant.37.clone.tables) | copy-start | bytes 6291460
  5.0 35.5 %copy-start.4 = (s32[13]{0:T(128)S(1)}, s32[13]{0:T(128)}, u32[]{:S(2)}) copy-start(s32[13]{0:T(128)} %concatenate.7.slip) | copy-start | bytes 160
  40.5 1.6 %copy-start.1 = (f32[4,1024,128]{2,1,0:T(8,128)S(1)}, f32[4,1024,128]{2,1,0:T(8,128)}, u32[]{:S(2)}) copy-start(f32[4,1024,128]{2,1,0:T(8,128)} %get-tuple-element.6) | copy-start | bytes 6291460
  42.1 0.8 copy-start.3
  114.8 1.3 %copy-start.2 = (f32[4,128,8,128]{3,2,1,0:T(8,128)}, f32[4,128,8,128]{3,2,1,0:T(8,128)S(1)}, u32[]{:S(2)}) copy-start(f32[4,128,8,128]{3,2,1,0:T(8,128)S(1)} %get-tuple-element.8) | copy-start | bytes 6291460
where the time goes:
time: 123 us; the launch traced here: 121 us
  Pallas kernels  110 us (89%)
  local copies, waits for them, and re-layouts  8.15 us (7%)
  other arithmetic  1.75 us (1%)
    pallas_call x1, Pallas kernels, on_device(): pl.pallas_call(filter_kernel, out_shape=(jax.ShapeDtypeStruct((4, DEVICES...  72 us
    pallas_call x1, Pallas kernels, on_device(): pl.pallas_call(steps_kernel, out_shape=(jax.ShapeDtypeStruct((4, DEVICES...  34.2 us
    unnamed x11, local copies, waits for them, and re-layouts  4.3 us
    pallas_call x1, Pallas kernels, on_device(): pl.pallas_call(unblock_kernel, grid=(4,), out_shape=jax.ShapeDtypeStruct(...  3.9 us

commit v1 on v0

v1 whole, which is shorter than its diff:
```python
import itertools

import jax
import jax.numpy as jnp
import numpy as np
from jax import lax
from jax.experimental import pallas as pl
from jax.experimental.pallas import tpu as pltpu
from jax.sharding import PartitionSpec as P

W = 256
HALF = 128
P_SIZE = 1024
STEPS = 4
NS = 512
CHAINS = 4
COARSE = 8
FINE = 16
DEVICES = COARSE * FINE
REACH = 10
GAIN = 0.25 * W * W / P_SIZE
SPREAD = 20.0
PARTS = 2
ROWS = 32 // PARTS
MESH = pl.DeviceIdType.MESH
f32, bf16 = jnp.float32, jnp.bfloat16


def halves(matrix):
    high = matrix.astype(np.float32).astype(bf16)
    low = (matrix - high.astype(np.float64)).astype(np.float32).astype(bf16)
    return high, low


def diffraction_tables():
    k = np.arange(W)
    signed = np.where(k < W // 2, k, k - W)
    h = np.exp(-1j * SPREAD * (2.0 * np.pi * signed / W) ** 2)
    q = np.fft.ifft(h)
    full = q[(k[:, None] - k[None, :]) % W]
    a, b = full[:HALF, :HALF], full[:HALF, HALF:]
    tables = []
    for part in (0.5 * (a + b), 0.5 * (a - b)):
        t = part.T
        tables.append(np.stack(halves(np.block([[t.real, t.imag], [-t.imag, t.real]]))))
    return np.stack(tables)


def place(n):
    n = lax.rem(n + 2 * DEVICES, DEVICES)
    return (n // FINE, lax.rem(n, FINE))


def far_first():
    offsets = [o for o in itertools.product(range(4), range(4), range(4), range(2)) if any(o)]
    mixed = np.random.RandomState(1).permutation(len(offsets))
    offsets = [offsets[i] for i in mixed]
    return sorted(offsets, key=lambda o: -sum(min(v, 4 - v) for v in o[:3]))


def partners():
    coarse, fine = lax.axis_index("coarse"), lax.axis_index("fine")
    x, y = fine // 4, coarse // 2
    z, core = (lax.rem(fine, 4) // 2) * 2 + lax.rem(coarse, 2), lax.rem(fine, 2)
    out = []
    for dx, dy, dz, dk in far_first():
        px, py, pz, pk = lax.rem(x + dx, 4), lax.rem(y + dy, 4), lax.rem(z + dz, 4), lax.rem(core + dk, 2)
        out.append((py * 2 + lax.rem(pz, 2), px * 4 + (pz // 2) * 2 + pk))
    return out


def sincos(x):
    turns = jnp.round(x * (2.0 / np.pi))
    r = x - turns * 1.5703125
    r = r - turns * 4.837512969970703125e-4
    r = r - turns * 7.54978995489188216e-8
    z = r * r
    sine = r + r * z * (-1.6666654611e-1 + z * (8.3321608736e-3 + z * -1.9515295891e-4))
    cosine = 1.0 - 0.5 * z + z * z * (4.166664568298827e-2 + z * (-1.388731625493765e-3 + z * 2.443315711809948e-5))
    quadrant = turns.astype(jnp.int32) & 3
    odd = (quadrant & 1) == 1
    s = jnp.where(odd, cosine, sine)
    c = jnp.where(odd, sine, cosine)
    s = jnp.where(quadrant >= 2, -s, s)
    c = jnp.where((quadrant == 1) | (quadrant == 2), -c, c)
    return s, c


def spline_rows(table, r, grid, cells, shifts):
    left = (0.5 * (0.5 - shifts) * (0.5 - shifts)).astype(bf16)
    middle = (0.75 - shifts * shifts).astype(bf16)
    right = (0.5 * (0.5 + shifts) * (0.5 + shifts)).astype(bf16)
    before = ((cells - 1) & (W - 1)).astype(f32).astype(bf16)
    after = ((cells + 1) & (W - 1)).astype(f32).astype(bf16)
    at = cells.astype(f32).astype(bf16)
    none = jnp.zeros((), bf16)
    for q in range(0, P_SIZE, W):
        lanes = slice(q, q + W)
        for row in range(0, W, 64):
            rows = grid[row : row + 64, :]
            value = jnp.where(rows == before[:, lanes], left[:, lanes], none)
            value = jnp.where(rows == at[:, lanes], middle[:, lanes], value)
            value = jnp.where(rows == after[:, lanes], right[:, lanes], value)
            table[r, row : row + 64, lanes] = value


def split(g):
    hi = g.astype(bf16)
    return hi, (g - hi.astype(f32)).astype(bf16)


def whole_kernel(
    plan, field_in, phases, energy, cells, shifts, bragg, matrices, back, particles,
    field, tx, ty, grid, gcells, gshifts, state, arrived, dep, cur, mright, mleft, lhs, rhs, rounded,
    sent, got, result, wave, turned, conv, operand, homes,
    field_sem, table_sem, gs, gr, ps, pr, own_sem, s1, r1, s2, r2, hs, hr,
):
    coarse, fine = lax.axis_index("coarse"), lax.axis_index("fine")
    me = coarse * FINE + fine
    others = partners()
    barrier = pltpu.get_barrier_semaphore()
    for there in others:
        pl.semaphore_signal(barrier, inc=1, device_id=there, device_id_type=MESH)
    slips = [plan[u] for u in range(STEPS)]
    met = [0]
    for u in range(STEPS):
        met.append(met[u] + slips[u])

    load = pltpu.make_async_copy(field_in, field, field_sem)
    load.start()
    tables = []
    for sy in range(2):
        for n, part in enumerate((0, 1, 0)):
            tables.append(pltpu.make_async_copy(
                matrices.at[sy, part], mright.at[sy, pl.ds(n * W, W)], table_sem.at[sy, n]))
        for n, part in enumerate((0, 0, 1)):
            for bx in range(2):
                for by in range(2):
                    tables.append(pltpu.make_async_copy(
                        matrices.at[sy, part, pl.ds(by * HALF, HALF), pl.ds(bx * HALF, HALF)],
                        mleft.at[sy, pl.ds(bx * HALF, HALF), pl.ds(n * W + by * HALF, HALF)],
                        table_sem.at[sy, 3 + n * 4 + bx * 2 + by]))
    for copy in tables:
        copy.start()
    grid[...] = lax.broadcasted_iota(jnp.int32, (W, W), 0).astype(f32).astype(bf16)

    def build(r, carry):
        spline_rows(tx, r, grid, gcells[r, 0:1, :], gshifts[r, 0:1, :])
        spline_rows(ty, r, grid, gcells[r, 1:2, :], gshifts[r, 1:2, :])
        return carry

    gcells[0:CHAINS] = cells[...]
    gshifts[0:CHAINS] = shifts[...]
    lax.fori_loop(0, CHAINS, build, 0)
    load.wait()
    for copy in tables:
        copy.wait()

    def advance(u, base, theta):
        sine, cosine = sincos(theta)
        for k in range(2):
            r = base + k + met[u]
            c, s = cosine[k : k + 1].astype(bf16), -sine[k : k + 1].astype(bf16)
            for row in range(0, W, 64):
                weights = tx[r, row : row + 64, :]
                dep[k, row : row + 64, :] = weights * c
                dep[k, W + row : W + row + 64, :] = weights * s
            cur[k] = lax.dot_general(dep[k], ty[r], (((1,), (1,)), ((), ())), preferred_element_type=f32)
        for k in range(2):
            chain = base + k
            at = me * CHAINS + chain
            keep = 1.0
            if u:
                keep = jnp.where((at + met[u] >= NS) & (at + met[u - 1] < NS), 0.0, 1.0)
            for c in range(2):
                for row in range(0, HALF, 32):
                    top = field[chain, c, row : row + 32, :] * keep + GAIN * cur[k, c * W + row : c * W + row + 32, :]
                    low = row + HALF
                    bottom = field[chain, c, low : low + 32, :] * keep + GAIN * cur[k, c * W + low : c * W + low + 32, :]
                    for sx, v in enumerate((top + bottom, top - bottom)):
                        a, b = v[:, :HALF], v[:, HALF:]
                        rows = slice(sx * HALF + row, sx * HALF + row + 32)
                        for sy, g in enumerate((a + b, a - b)):
                            hi, lo = split(g)
                            lhs[k, sy, rows, c * HALF : c * HALF + HALF] = hi
                            lhs[k, sy, rows, W + c * HALF : W + c * HALF + HALF] = hi
                            lhs[k, sy, rows, 2 * W + c * HALF : 2 * W + c * HALF + HALF] = lo
            for sy in range(2):
                mid = jnp.dot(lhs[k, sy], mright[sy], preferred_element_type=f32)
                for sx in range(2):
                    for c in range(2):
                        hi, lo = split(mid[sx * HALF : sx * HALF + HALF, c * HALF : c * HALF + HALF])
                        cols = slice(sy * HALF, sy * HALF + HALF)
                        rhs[k, sx, c * HALF : c * HALF + HALF, cols] = hi
                        rhs[k, sx, W + c * HALF : W + c * HALF + HALF, cols] = lo
                        rhs[k, sx, 2 * W + c * HALF : 2 * W + c * HALF + HALF, cols] = hi
        for k in range(2):
            chain = base + k
            at = me * CHAINS + chain
            za = jnp.dot(mleft[0], rhs[k, 0], preferred_element_type=f32)
            zb = jnp.dot(mleft[1], rhs[k, 1], preferred_element_type=f32)
            for c in range(2):
                p, n = za[c * HALF : c * HALF + HALF], zb[c * HALF : c * HALF + HALF]
                for hx, v in enumerate((p + n, p - n)):
                    a, b = v[:, :HALF], v[:, HALF:]
                    for hy, g in enumerate((a + b, a - b)):
                        cols = slice(hy * HALF, hy * HALF + HALF)
                        rounded[chain, c * W + hx * HALF : c * W + hx * HALF + HALF, cols] = g.astype(bf16)
                        if u < STEPS - 1:
                            field[chain, c, hx * HALF : hx * HALF + HALF, cols] = g
                        else:
                            gone = (at + met[STEPS] >= NS) & (at + met[STEPS - 1] < NS)
                            row = (2 * hx + hy) * 8 + c * CHAINS + chain
                            sent[pl.ds(row, HALF, stride=32), :] = g * jnp.where(gone, 0.0, 1.0)
        return sine, cosine

    def push(u, base, theta, eta, sine, cosine):
        sampled = []
        for k in range(2):
            r = base + k + met[u]
            pieces = []
            for q in range(0, P_SIZE, 256):
                picked = jnp.dot(rounded[base + k], ty[r, :, q : q + 256], preferred_element_type=f32)
                weights = tx[r, :, q : q + 256].astype(f32)
                pieces.append([jnp.sum(picked[c * W : c * W + W] * weights, axis=0, keepdims=True) for c in range(2)])
            sampled.append([jnp.concatenate([piece[c] for piece in pieces], axis=1) for c in range(2)])
        first = jnp.concatenate([sampled[0][0], sampled[1][0]], axis=0)
        second = jnp.concatenate([sampled[0][1], sampled[1][1]], axis=0)
        eta = eta - 0.5 * (first * cosine - second * sine)
        state[u, 0, base : base + 2, :] = theta + eta
        state[u, 1, base : base + 2, :] = eta

    def exchange(u):
        return [
            pltpu.make_async_remote_copy(
                state.at[u, n, pl.ds(0, 2)], arrived.at[u, n], ps.at[u, n], pr.at[u, n],
                device_id=place(me - 1), device_id_type=MESH)
            for n in range(2)
        ]

    geometry = []
    for n, (src, dst) in enumerate(((cells, gcells), (shifts, gshifts))):
        geometry.append(pltpu.make_async_remote_copy(
            src, dst.at[pl.ds(4, 4)], gs.at[n], gr.at[n], device_id=place(me - 1), device_id_type=MESH))
        geometry.append(pltpu.make_async_remote_copy(
            src.at[pl.ds(0, 2)], dst.at[pl.ds(8, 2)], gs.at[n + 2], gr.at[n + 2],
            device_id=place(me - 2), device_id_type=MESH))

    def front(u):
        if not u:
            return phases[0:2], energy[0:2]
        one = slips[u - 1] == 1
        return [jnp.where(one, state[u - 1, n, 1:3, :], state[u - 1, n, 2:4, :]) for n in range(2)]

    def rear(u):
        if not u:
            return phases[2:4], energy[2:4]
        one = slips[u - 1] == 1
        return [
            jnp.where(
                one,
                jnp.concatenate([state[u - 1, n, 3:4, :], arrived[u - 1, n, 0:1, :]], axis=0),
                arrived[u - 1, n],
            )
            for n in range(2)
        ]

    moving = []
    for u in range(STEPS - 1):
        theta, eta = front(u)
        push(u, 0, theta, eta, *advance(u, 0, theta))
        if u == 0:
            pl.semaphore_wait(barrier, DEVICES - 1)
            for copy in geometry:
                copy.start()
        for copy in moving:
            copy.wait()
        if u == 1:
            for copy in geometry:
                copy.wait()
            lax.fori_loop(CHAINS, REACH, build, 0)
        moving = exchange(u)
        for copy in moving:
            copy.start()
        theta, eta = rear(u)
        push(u, 2, theta, eta, *advance(u, 2, theta))
    last = STEPS - 1
    ahead = front(last)
    ahead_turn = advance(last, 0, ahead[0])
    for copy in moving:
        copy.wait()
    behind = rear(last)
    behind_turn = advance(last, 2, behind[0])

    def spread(src, dst, q, ss, rs):
        for there in others:
            n = there[0] * FINE + there[1]
            pltpu.make_async_remote_copy(
                src.at[pl.ds(n * 32 + q * ROWS, ROWS)], dst.at[pl.ds(me * 32 + q * ROWS, ROWS)], ss.at[q], rs.at[q],
                device_id=there, device_id_type=MESH).start()

    def settle(ref, q, sem):
        view = ref.at[pl.ds(0, (DEVICES - 1) * ROWS)]
        pltpu.make_async_copy(view, view, sem.at[q]).wait()

    for q in range(PARTS):
        spread(sent, got, q, s1, r1)
    mine = pl.ds(pl.multiple_of(me * 32, 32), 32)
    got[mine, :] = sent[mine, :]
    push(last, 0, *ahead, *ahead_turn)
    push(last, 2, *behind, *behind_turn)
    homing = [
        pltpu.make_async_remote_copy(
            state.at[last], homes.at[n], hs.at[n], hr.at[n], device_id=place(me + n + 1), device_id_type=MESH)
        for n in range(2)
    ]
    for copy in homing:
        copy.start()

    half = NS // 2
    k = lax.broadcasted_iota(jnp.int32, (1, NS), 1)
    unit = 2.0 * np.pi / NS
    turn_quad, turn_real = sincos(((k * met[STEPS]) & (NS - 1)).astype(f32) * unit)
    br, bi = bragg[0:1, :] * (1.0 / NS), bragg[1:2, :] * (1.0 / NS)
    response = jnp.concatenate([br * turn_real + bi * turn_quad, bi * turn_real - br * turn_quad], axis=0)
    hi, rest = response.astype(bf16), None
    rest = response - hi.astype(f32)
    lo = rest.astype(bf16)
    tiny = (rest - lo.astype(f32)).astype(bf16)
    down = lax.broadcasted_iota(jnp.int32, (NS, NS), 0)
    across = lax.broadcasted_iota(jnp.int32, (NS, NS), 1)
    picks = jnp.where(down == ((2 * across) & (NS - 1)) + (across >> 8), 1.0, 0.0).astype(bf16)
    ordered = (
        jnp.dot(hi, picks, preferred_element_type=f32)
        + jnp.dot(lo, picks, preferred_element_type=f32)
        + jnp.dot(tiny, picks, preferred_element_type=f32)
    )
    for parity in range(2):
        real = ordered[0:1, parity * half : parity * half + half]
        quad = ordered[1:2, parity * half : parity * half + half]

        def fill(block, carry, parity=parity, real=real, quad=quad):
            start = pl.multiple_of(block * 32, 32)
            row = lax.broadcasted_iota(jnp.int32, (32, half), 0) + start
            m = lax.broadcasted_iota(jnp.int32, (32, half), 1)
            time = (row >> 3) * 4 + (row & 3)
            upper = (row & 4) == 0
            s, c = sincos((((2 * m + parity) * time) & (NS - 1)).astype(f32) * unit)
            wr = jnp.where(upper, c, s)
            wi = jnp.where(upper, -s, c)
            for n, (w, g) in enumerate(((wr, wr * real + wi * quad), (wi, wi * real - wr * quad))):
                cols = slice(n * half, n * half + half)
                hi, lo = split(w)
                wave[0, pl.ds(start, 32), cols] = hi
                wave[1, pl.ds(start, 32), cols] = lo
                hi, lo = split(g)
                turned[0, pl.ds(start, 32), cols] = hi
                turned[1, pl.ds(start, 32), cols] = lo
            return carry

        lax.fori_loop(0, NS // 32, fill, 0)
        dims = (((1,), (1,)), ((), ()))
        for row in range(0, NS, 256):
            rows = slice(row, row + 256)
            kernel = (
                lax.dot_general(turned[0, rows], wave[0], dims, preferred_element_type=f32)
                + lax.dot_general(turned[0, rows], wave[1], dims, preferred_element_type=f32)
                + lax.dot_general(turned[1, rows], wave[0], dims, preferred_element_type=f32)
            )
            hi, lo = split(kernel)
            conv[parity, rows, 0:NS] = hi
            conv[parity, rows, NS : 2 * NS] = hi
            conv[parity, rows, 2 * NS : 3 * NS] = lo

    mid = DEVICES // 2
    tiles = 4 // PARTS
    for q in range(PARTS):
        settle(got, q, r1)
        for tile in range(tiles):
            lanes = slice(tile * HALF, tile * HALF + HALF)
            for block in range(0, mid, 8):
                rows = block * 8
                pieces = []
                for start in (block, mid + block):
                    pieces.append(jnp.concatenate(
                        [got[(start + n) * 32 + (q * tiles + tile) * 8 : (start + n) * 32 + (q * tiles + tile) * 8 + 8, :] for n in range(8)],
                        axis=0))
                a, b = pieces
                for parity, g in enumerate((a + b, a - b)):
                    hi, lo = split(g)
                    operand[parity, rows : rows + 64, lanes] = hi
                    operand[parity, NS + rows : NS + rows + 64, lanes] = lo
                    operand[parity, 2 * NS + rows : 2 * NS + rows + 64, lanes] = hi
        for block in range(0, NS, 256):
            even = jnp.dot(conv[0, block : block + 256, :], operand[0], preferred_element_type=f32)
            odd = jnp.dot(conv[1, block : block + 256, :], operand[1], preferred_element_type=f32)
            total, gap = even + odd, even - odd
            for tile in range(tiles):
                lanes = slice(tile * HALF, tile * HALF + HALF)
                for n in range(32):
                    to = (block // 8 + n) * 32 + (q * tiles + tile) * 8
                    result[to : to + 8, :] = total[n * 8 : n * 8 + 8, lanes]
                    result[mid * 32 + to : mid * 32 + to + 8, :] = gap[n * 8 : n * 8 + 8, lanes]
        spread(result, back, q, s2, r2)
    own = pltpu.make_async_copy(result.at[mine], back.at[mine], own_sem)
    own.start()
    for copy in homing:
        copy.wait()
    for i in range(CHAINS):
        at = i - met[last]
        for n in range(2):
            value = homes[1, n, pl.ds(jnp.clip(at + 8, 0, 3), 1), :]
            value = jnp.where(at >= -4, homes[0, n, pl.ds(jnp.clip(at + 4, 0, 3), 1), :], value)
            value = jnp.where(at >= 0, state[last, n, pl.ds(jnp.clip(at, 0, 3), 1), :], value)
            particles[i, n : n + 1, :] = value
    own.wait()
    for q in range(PARTS):
        settle(got, q, s1)
        settle(got, q, s2)
        settle(got, q, r2)


def unblock_kernel(blocks, out, staged, sems):
    copies = []
    for chain in range(CHAINS):
        for c in range(2):
            for hx in range(2):
                for hy in range(2):
                    staged[chain, c, hx * HALF : hx * HALF + HALF, hy * HALF : hy * HALF + HALF] = blocks[
                        pl.ds((2 * hx + hy) * 8 + c * CHAINS + chain, HALF, stride=32), :
                    ]
        copy = pltpu.make_async_copy(staged.at[chain], out.at[chain], sems.at[chain])
        copy.start()
        copies.append(copy)
    for copy in copies:
        copy.wait()


def on_device(field_in, phases, energy, cell_index, offsets, slip_plan, bragg_response):
    vmem = pl.BlockSpec(memory_space=pltpu.VMEM)
    smem = pl.BlockSpec(memory_space=pltpu.SMEM)
    whole = pl.BlockSpec(memory_space=pl.ANY)
    dma = pltpu.SemaphoreType.DMA
    back, particles = pl.pallas_call(
        whole_kernel,
        out_shape=(
            jax.ShapeDtypeStruct((DEVICES * 32, HALF), f32),
            jax.ShapeDtypeStruct((CHAINS, 2, P_SIZE), f32),
        ),
        in_specs=[smem, whole, vmem, vmem, vmem, vmem, vmem, whole],
        out_specs=(whole, vmem),
        scratch_shapes=[
            pltpu.VMEM((CHAINS, 2, W, W), f32),
            pltpu.VMEM((REACH, W, P_SIZE), bf16),
            pltpu.VMEM((REACH, W, P_SIZE), bf16),
            pltpu.VMEM((W, W), bf16),
            pltpu.VMEM((REACH, 2, P_SIZE), jnp.int32),
            pltpu.VMEM((REACH, 2, P_SIZE), f32),
            pltpu.VMEM((STEPS, 2, CHAINS, P_SIZE), f32),
            pltpu.VMEM((STEPS, 2, 2, P_SIZE), f32),
            pltpu.VMEM((2, 2 * W, P_SIZE), bf16),
            pltpu.VMEM((2, 2 * W, W), f32),
            pltpu.VMEM((2, 3 * W, W), bf16),
            pltpu.VMEM((2, W, 3 * W), bf16),
            pltpu.VMEM((2, 2, W, 3 * W), bf16),
            pltpu.VMEM((2, 2, 3 * W, W), bf16),
            pltpu.VMEM((CHAINS, 2 * W, W), bf16),
            pltpu.VMEM((DEVICES * 32, HALF), f32),
            pltpu.VMEM((DEVICES * 32, HALF), f32),
            pltpu.VMEM((DEVICES * 32, HALF), f32),
            pltpu.VMEM((2, NS, NS), bf16),
            pltpu.VMEM((2, NS, NS), bf16),
            pltpu.VMEM((2, NS, 3 * NS), bf16),
            pltpu.VMEM((2, 3 * NS, 2 * W // PARTS), bf16),
            pltpu.VMEM((2, 2, CHAINS, P_SIZE), f32),
            dma,
            dma((2, 15)),
            dma((4,)),
            dma((4,)),
            dma((STEPS, 2)),
            dma((STEPS, 2)),
            dma,
            dma((PARTS,)),
            dma((PARTS,)),
            dma((PARTS,)),
            dma((PARTS,)),
            dma((2,)),
            dma((2,)),
        ],
        compiler_params=pltpu.CompilerParams(
            collective_id=0, has_side_effects=True, vmem_limit_bytes=52 << 20
        ),
        name="pass",
    )(slip_plan, field_in, phases, energy, cell_index, offsets, bragg_response, jnp.asarray(diffraction_tables()))
    field_out = pl.pallas_call(
        unblock_kernel,
        out_shape=jax.ShapeDtypeStruct((CHAINS, 2, W, W), f32),
        in_specs=[vmem],
        out_specs=whole,
        scratch_shapes=[pltpu.VMEM((CHAINS, 2, W, W), f32), dma((CHAINS,))],
        compiler_params=pltpu.CompilerParams(vmem_limit_bytes=8 << 20),
        name="unblock",
    )(back)
    return field_out, particles


def solution(mesh):
    axes = ("coarse", "fine")
    in_specs = (
        P(axes, None, None, None),
        P(axes, None),
        P(axes, None),
        P(axes, None, None),
        P(axes, None, None),
        P(),
        P(),
    )
    out_specs = (P(axes, None, None, None), P(axes, None, None))
    return jax.shard_map(on_device, mesh=mesh, in_specs=in_specs, out_specs=out_specs, check_vma=False)
```

time: 123 us -> 101 us (0.82)
  the two profiles are of different devices: /device:TPU:35 before, /device:TPU:3 now
where the time goes in v1:
time: 101 us
  Pallas kernels  92.7 us (92%)
  local copies, waits for them, and re-layouts  7.53 us (7%)
    pallas_call x1, Pallas kernels, on_device(): pl.pallas_call(whole_kernel, out_shape=(jax.ShapeDtypeStruct((DEVICES * 3...  90.2 us
    unnamed x17, local copies, waits for them, and re-layouts  7.53 us
    pallas_call x1, Pallas kernels, on_device(): pl.pallas_call(unblock_kernel, out_shape=jax.ShapeDtypeStruct((CHAINS, 2,...  2.48 us

profile of v1, /device:TPU:3, one launch (start us, length us, event | category | flops | bytes accessed | tf_op | source)
XLA Modules:
  0.0 100.9 jit_solution(17676950037314448341)
XLA Ops:
  0.6 0.0 copy-start.1
  0.6 1.0 %copy-done.1 = bf16[2,2,256,256]{3,2,1,0:T(8,128)(2,1)S(1)} copy-done((bf16[2,2,256,256]{3,2,1,0:T(8,128)(2,1)S(1)}, bf16[2,2,256,256]{3,2,1,0:T(8,128)(2,1)}, u32[]{:S(2)}) %copy-start.1) | copy-done | bytes 524312
  1.7 0.0 copy-start.2
  1.7 0.8 copy-done.2
  2.4 0.0 copy-start.3
  2.4 0.8 copy-done.3
  3.2 0.0 copy-start.4
  3.2 0.7 copy-done.4
  3.9 0.0 copy-start.5
  3.9 0.7 copy-done.5
  4.6 0.0 copy-start.6
  4.6 0.7 copy-done.6
  5.3 0.0 copy-start.7
  5.3 0.7 copy-done.7
  6.0 90.2 %pass.1 = (f32[4096,128]{1,0:T(8,128)}, f32[4,2,1024]{2,1,0:T(2,128)S(1)}) custom-call(s32[4]{0:T(128)S(1)} %copy-done.7, f32[4,2,256,256]{3,2,1,0:T(8,128)} %field_in.1, f32[4,1024]{1,0:T(4,128)S(1)} %copy-done.4, f32[4,1024]{1,0:T(4,128)S(1)} %copy-done.5, s32[4,2,1024]{2,1,0:T(2,128)S(1)} %copy-done.2, f32[4,2,1024]{2,1,0:T(2,128)S(1)} %copy-done.3, ...), custom_call_target="tpu_custom_call" | custom-call | tf_op jit(solution)/shard_map/pass/pallas_call | solution.py:444
  96.2 0.0 copy-start
  96.2 1.6 %copy-done = f32[4096,128]{1,0:T(8,128)S(1)} copy-done((f32[4096,128]{1,0:T(8,128)S(1)}, f32[4096,128]{1,0:T(8,128)}, u32[]{:S(2)}) %copy-start) | copy-done | bytes 2097176
  97.7 2.5 %unblock.1 = f32[4,2,256,256]{3,2,1,0:T(8,128)} custom-call(f32[4096,128]{1,0:T(8,128)S(1)} %copy-done), custom_call_target="tpu_custom_call" | custom-call | tf_op jit(solution)/shard_map/unblock/pallas_call | solution.py:495
  100.2 0.6 copy.11
Async XLA Ops:
  0.6 1.0 %copy-start.1 = (bf16[2,2,256,256]{3,2,1,0:T(8,128)(2,1)S(1)}, bf16[2,2,256,256]{3,2,1,0:T(8,128)(2,1)}, u32[]{:S(2)}) copy-start(bf16[2,2,256,256]{3,2,1,0:T(8,128)(2,1)} %constant.2.clone.matrices) | copy-start | bytes 1572868
  1.7 0.8 copy-start.2
  2.4 0.8 copy-start.3
  3.2 0.7 copy-start.4
  3.9 0.7 copy-start.5
  4.6 0.7 copy-start.6
  5.3 0.7 copy-start.7
  96.2 1.6 %copy-start = (f32[4096,128]{1,0:T(8,128)S(1)}, f32[4096,128]{1,0:T(8,128)}, u32[]{:S(2)}) copy-start(f32[4096,128]{1,0:T(8,128)} %get-tuple-element.4.blocks) | copy-start | bytes 6291460

commit v2 on v1

--- a/solution.py
+++ b/solution.py
@@ -20,8 +20,7 @@
 REACH = 10
 GAIN = 0.25 * W * W / P_SIZE
 SPREAD = 20.0
-PARTS = 2
-ROWS = 32 // PARTS
+VMEM_ALL = 67043328
 MESH = pl.DeviceIdType.MESH
 f32, bf16 = jnp.float32, jnp.bfloat16
 
@@ -110,22 +109,26 @@
 
 
 def whole_kernel(
-    plan, field_in, phases, energy, cells, shifts, bragg, matrices, back, particles,
-    field, tx, ty, grid, gcells, gshifts, state, arrived, dep, cur, mright, mleft, lhs, rhs, rounded,
+    plan, field_in, phases_in, energy_in, cells_in, shifts_in, bragg_in, matrices, back, particles,
+    phases, energy, cells, shifts, bragg, field, tx, ty, grid, gcells, gshifts, state, arrived, dep, cur, mright, mleft, lhs, rhs, rounded,
     sent, got, result, wave, turned, conv, operand, homes,
-    field_sem, table_sem, gs, gr, ps, pr, own_sem, s1, r1, s2, r2, hs, hr,
+    small_sem, field_sem, table_sem, gs, gr, ps, pr, own_sem, s1, r1, s2, r2, hs, hr,
 ):
     coarse, fine = lax.axis_index("coarse"), lax.axis_index("fine")
     me = coarse * FINE + fine
     others = partners()
-    barrier = pltpu.get_barrier_semaphore()
-    for there in others:
-        pl.semaphore_signal(barrier, inc=1, device_id=there, device_id_type=MESH)
     slips = [plan[u] for u in range(STEPS)]
     met = [0]
     for u in range(STEPS):
         met.append(met[u] + slips[u])
 
+    small = [
+        pltpu.make_async_copy(src, dst, small_sem.at[n])
+        for n, (src, dst) in enumerate((
+            (cells_in, cells), (shifts_in, shifts), (phases_in, phases), (energy_in, energy), (bragg_in, bragg)))
+    ]
+    for copy in small:
+        copy.start()
     load = pltpu.make_async_copy(field_in, field, field_sem)
     load.start()
     tables = []
@@ -142,6 +145,9 @@
                         table_sem.at[sy, 3 + n * 4 + bx * 2 + by]))
     for copy in tables:
         copy.start()
+    barrier = pltpu.get_barrier_semaphore()
+    for there in others:
+        pl.semaphore_signal(barrier, inc=1, device_id=there, device_id_type=MESH)
     grid[...] = lax.broadcasted_iota(jnp.int32, (W, W), 0).astype(f32).astype(bf16)
 
     def build(r, carry):
@@ -149,6 +155,8 @@
         spline_rows(ty, r, grid, gcells[r, 1:2, :], gshifts[r, 1:2, :])
         return carry
 
+    for copy in small:
+        copy.wait()
     gcells[0:CHAINS] = cells[...]
     gshifts[0:CHAINS] = shifts[...]
     lax.fori_loop(0, CHAINS, build, 0)
@@ -210,8 +218,7 @@
                             field[chain, c, hx * HALF : hx * HALF + HALF, cols] = g
                         else:
                             gone = (at + met[STEPS] >= NS) & (at + met[STEPS - 1] < NS)
-                            row = (2 * hx + hy) * 8 + c * CHAINS + chain
-                            sent[pl.ds(row, HALF, stride=32), :] = g * jnp.where(gone, 0.0, 1.0)
+                            sent[base + hy, pl.ds(hx * 4 + c * 2 + k, HALF, stride=8), :] = g * jnp.where(gone, 0.0, 1.0)
         return sine, cosine
 
     def push(u, base, theta, eta, sine, cosine):
@@ -285,28 +292,30 @@
         theta, eta = rear(u)
         push(u, 2, theta, eta, *advance(u, 2, theta))
     last = STEPS - 1
+    def spread(src, dst, first, count, ss, rs):
+        parts = pl.ds(first, count)
+        for there in others:
+            n = there[0] * FINE + there[1]
+            pltpu.make_async_remote_copy(
+                src.at[parts, pl.ds(n * 8, 8)], dst.at[parts, pl.ds(me * 8, 8)], ss, rs,
+                device_id=there, device_id_type=MESH).start()
+
+    def settle(ref, count, sem):
+        view = ref.at[pl.ds(0, count), pl.ds(0, (DEVICES - 1) * 8)]
+        pltpu.make_async_copy(view, view, sem).wait()
+
     ahead = front(last)
     ahead_turn = advance(last, 0, ahead[0])
+    spread(sent, got, 0, 2, s1.at[0], r1.at[0])
     for copy in moving:
         copy.wait()
     behind = rear(last)
     behind_turn = advance(last, 2, behind[0])
-
-    def spread(src, dst, q, ss, rs):
-        for there in others:
-            n = there[0] * FINE + there[1]
-            pltpu.make_async_remote_copy(
-                src.at[pl.ds(n * 32 + q * ROWS, ROWS)], dst.at[pl.ds(me * 32 + q * ROWS, ROWS)], ss.at[q], rs.at[q],
-                device_id=there, device_id_type=MESH).start()
-
-    def settle(ref, q, sem):
-        view = ref.at[pl.ds(0, (DEVICES - 1) * ROWS)]
-        pltpu.make_async_copy(view, view, sem.at[q]).wait()
-
-    for q in range(PARTS):
-        spread(sent, got, q, s1, r1)
-    mine = pl.ds(pl.multiple_of(me * 32, 32), 32)
-    got[mine, :] = sent[mine, :]
+    spread(sent, got, 2, 1, s1.at[1], r1.at[1])
+    spread(sent, got, 3, 1, s1.at[2], r1.at[2])
+    mine = pl.ds(pl.multiple_of(me * 8, 8), 8)
+    for part in range(4):
+        got[part, mine, :] = sent[part, mine, :]
     push(last, 0, *ahead, *ahead_turn)
     push(last, 2, *behind, *behind_turn)
     homing = [
@@ -343,8 +352,8 @@
             start = pl.multiple_of(block * 32, 32)
             row = lax.broadcasted_iota(jnp.int32, (32, half), 0) + start
             m = lax.broadcasted_iota(jnp.int32, (32, half), 1)
-            time = (row >> 3) * 4 + (row & 3)
-            upper = (row & 4) == 0
+            time = (row >> 3) * 4 + ((row >> 2) & 1) * 2 + (row & 1)
+            upper = (row & 2) == 0
             s, c = sincos((((2 * m + parity) * time) & (NS - 1)).astype(f32) * unit)
             wr = jnp.where(upper, c, s)
             wi = jnp.where(upper, -s, c)
@@ -373,36 +382,37 @@
             conv[parity, rows, 2 * NS : 3 * NS] = lo
 
     mid = DEVICES // 2
-    tiles = 4 // PARTS
-    for q in range(PARTS):
-        settle(got, q, r1)
-        for tile in range(tiles):
-            lanes = slice(tile * HALF, tile * HALF + HALF)
-            for block in range(0, mid, 8):
+    low = lax.broadcasted_iota(jnp.int32, (8, 8, HALF), 1) < 4
+    settle(got, 2, r1.at[0])
+    for hy in range(2):
+        settle(got, 1, r1.at[1 + hy])
+        for block in range(0, mid, 8):
+            pieces = []
+            for start in (block, mid + block):
+                a = got[hy, start * 8 : start * 8 + 64, :].reshape(8, 8, HALF)
+                b = got[2 + hy, start * 8 : start * 8 + 64, :].reshape(8, 8, HALF)
+                pieces.append((
+                    jnp.where(low, a, pltpu.roll(b, 4, 1)).reshape(64, HALF),
+                    jnp.where(low, pltpu.roll(a, 4, 1), b).reshape(64, HALF),
+                ))
+            for hx in range(2):
+                a, b = pieces[0][hx], pieces[1][hx]
+                lanes = slice(hx * HALF, hx * HALF + HALF)
                 rows = block * 8
-                pieces = []
-                for start in (block, mid + block):
-                    pieces.append(jnp.concatenate(
-                        [got[(start + n) * 32 + (q * tiles + tile) * 8 : (start + n) * 32 + (q * tiles + tile) * 8 + 8, :] for n in range(8)],
-                        axis=0))
-                a, b = pieces
                 for parity, g in enumerate((a + b, a - b)):
                     hi, lo = split(g)
                     operand[parity, rows : rows + 64, lanes] = hi
                     operand[parity, NS + rows : NS + rows + 64, lanes] = lo
                     operand[parity, 2 * NS + rows : 2 * NS + rows + 64, lanes] = hi
-        for block in range(0, NS, 256):
-            even = jnp.dot(conv[0, block : block + 256, :], operand[0], preferred_element_type=f32)
-            odd = jnp.dot(conv[1, block : block + 256, :], operand[1], preferred_element_type=f32)
-            total, gap = even + odd, even - odd
-            for tile in range(tiles):
-                lanes = slice(tile * HALF, tile * HALF + HALF)
-                for n in range(32):
-                    to = (block // 8 + n) * 32 + (q * tiles + tile) * 8
-                    result[to : to + 8, :] = total[n * 8 : n * 8 + 8, lanes]
-                    result[mid * 32 + to : mid * 32 + to + 8, :] = gap[n * 8 : n * 8 + 8, lanes]
-        spread(result, back, q, s2, r2)
-    own = pltpu.make_async_copy(result.at[mine], back.at[mine], own_sem)
+        for row in range(0, NS, 256):
+            even = jnp.dot(conv[0, row : row + 256, :], operand[0], preferred_element_type=f32)
+            odd = jnp.dot(conv[1, row : row + 256, :], operand[1], preferred_element_type=f32)
+            for hx in range(2):
+                a, b = even[:, hx * HALF : hx * HALF + HALF], odd[:, hx * HALF : hx * HALF + HALF]
+                result[2 * hy + hx, row : row + 256, :] = a + b
+                result[2 * hy + hx, mid * 8 + row : mid * 8 + row + 256, :] = a - b
+        spread(result, back, 2 * hy, 2, s2.at[hy], r2.at[hy])
+    own = pltpu.make_async_copy(result.at[:, mine], back.at[:, mine], own_sem)
     own.start()
     for copy in homing:
         copy.wait()
@@ -414,26 +424,43 @@
             value = jnp.where(at >= 0, state[last, n, pl.ds(jnp.clip(at, 0, 3), 1), :], value)
             particles[i, n : n + 1, :] = value
     own.wait()
-    for q in range(PARTS):
-        settle(got, q, s1)
-        settle(got, q, s2)
-        settle(got, q, r2)
-
-
-def unblock_kernel(blocks, out, staged, sems):
-    copies = []
-    for chain in range(CHAINS):
-        for c in range(2):
-            for hx in range(2):
-                for hy in range(2):
-                    staged[chain, c, hx * HALF : hx * HALF + HALF, hy * HALF : hy * HALF + HALF] = blocks[
-                        pl.ds((2 * hx + hy) * 8 + c * CHAINS + chain, HALF, stride=32), :
-                    ]
-        copy = pltpu.make_async_copy(staged.at[chain], out.at[chain], sems.at[chain])
+    for n, count in enumerate((2, 1, 1)):
+        settle(got, count, s1.at[n])
+    for hy in range(2):
+        settle(got, 2, s2.at[hy])
+        settle(got, 2, r2.at[hy])
+
+
+def unblock_kernel(blocks, ended, out, particles, taken, staged, kept, take_sems, put_sems, end_sems):
+    near, rows = [], 2 * HALF
+    for q in range(4):
+        near.append(pltpu.make_async_copy(
+            blocks.at[:, pl.ds(q * rows, rows)], taken.at[:, pl.ds(q * rows, rows)], take_sems.at[q]))
+    ends = pltpu.make_async_copy(ended, kept, end_sems.at[0])
+    for copy in near:
         copy.start()
-        copies.append(copy)
-    for copy in copies:
+    ends.start()
+    puts = []
+    for q in range(4):
+        near[q].wait()
+        if q == 0:
+            ends.wait()
+            ends = pltpu.make_async_copy(kept, particles, end_sems.at[1])
+            ends.start()
+        for chain in range(CHAINS):
+            for c in range(2):
+                row = (chain // 2) * 4 + c * 2 + chain % 2
+                for hx in range(2):
+                    for hy in range(2):
+                        staged[chain, c, hx, q * 32 : q * 32 + 32, hy * HALF : hy * HALF + HALF] = taken[
+                            2 * hy + hx, pl.ds(q * rows + row, 32, stride=8), :
+                        ]
+        puts.append(pltpu.make_async_copy(
+            staged.at[:, :, :, pl.ds(q * 32, 32)], out.at[:, :, :, pl.ds(q * 32, 32)], put_sems.at[q]))
+        puts[q].start()
+    for copy in puts:
         copy.wait()
+    ends.wait()
 
 
 def on_device(field_in, phases, energy, cell_index, offsets, slip_plan, bragg_response):
@@ -441,15 +468,21 @@
     smem = pl.BlockSpec(memory_space=pltpu.SMEM)
     whole = pl.BlockSpec(memory_space=pl.ANY)
     dma = pltpu.SemaphoreType.DMA
-    back, particles = pl.pallas_call(
+    far = pl.BlockSpec(memory_space=pltpu.HBM)
+    back, ended = pl.pallas_call(
         whole_kernel,
         out_shape=(
-            jax.ShapeDtypeStruct((DEVICES * 32, HALF), f32),
+            jax.ShapeDtypeStruct((4, DEVICES * 8, HALF), f32),
             jax.ShapeDtypeStruct((CHAINS, 2, P_SIZE), f32),
         ),
-        in_specs=[smem, whole, vmem, vmem, vmem, vmem, vmem, whole],
+        in_specs=[smem] + [far] * 7,
         out_specs=(whole, vmem),
         scratch_shapes=[
+            pltpu.VMEM((CHAINS, P_SIZE), f32),
+            pltpu.VMEM((CHAINS, P_SIZE), f32),
+            pltpu.VMEM((CHAINS, 2, P_SIZE), jnp.int32),
+            pltpu.VMEM((CHAINS, 2, P_SIZE), f32),
+            pltpu.VMEM((2, NS), f32),
             pltpu.VMEM((CHAINS, 2, W, W), f32),
             pltpu.VMEM((REACH, W, P_SIZE), bf16),
             pltpu.VMEM((REACH, W, P_SIZE), bf16),
@@ -465,14 +498,15 @@
             pltpu.VMEM((2, 2, W, 3 * W), bf16),
             pltpu.VMEM((2, 2, 3 * W, W), bf16),
             pltpu.VMEM((CHAINS, 2 * W, W), bf16),
-            pltpu.VMEM((DEVICES * 32, HALF), f32),
-            pltpu.VMEM((DEVICES * 32, HALF), f32),
-            pltpu.VMEM((DEVICES * 32, HALF), f32),
+            pltpu.VMEM((4, DEVICES * 8, HALF), f32),
+            pltpu.VMEM((4, DEVICES * 8, HALF), f32),
+            pltpu.VMEM((4, DEVICES * 8, HALF), f32),
             pltpu.VMEM((2, NS, NS), bf16),
             pltpu.VMEM((2, NS, NS), bf16),
             pltpu.VMEM((2, NS, 3 * NS), bf16),
-            pltpu.VMEM((2, 3 * NS, 2 * W // PARTS), bf16),
+            pltpu.VMEM((2, 3 * NS, W), bf16),
             pltpu.VMEM((2, 2, CHAINS, P_SIZE), f32),
+            dma((5,)),
             dma,
             dma((2, 15)),
             dma((4,)),
@@ -480,28 +514,38 @@
             dma((STEPS, 2)),
             dma((STEPS, 2)),
             dma,
-            dma((PARTS,)),
-            dma((PARTS,)),
-            dma((PARTS,)),
-            dma((PARTS,)),
+            dma((3,)),
+            dma((3,)),
+            dma((2,)),
+            dma((2,)),
             dma((2,)),
             dma((2,)),
         ],
         compiler_params=pltpu.CompilerParams(
-            collective_id=0, has_side_effects=True, vmem_limit_bytes=52 << 20
+            collective_id=0, has_side_effects=True, vmem_limit_bytes=VMEM_ALL
         ),
         name="pass",
     )(slip_plan, field_in, phases, energy, cell_index, offsets, bragg_response, jnp.asarray(diffraction_tables()))
-    field_out = pl.pallas_call(
+    field_out, particles = pl.pallas_call(
         unblock_kernel,
-        out_shape=jax.ShapeDtypeStruct((CHAINS, 2, W, W), f32),
-        in_specs=[vmem],
-        out_specs=whole,
-        scratch_shapes=[pltpu.VMEM((CHAINS, 2, W, W), f32), dma((CHAINS,))],
-        compiler_params=pltpu.CompilerParams(vmem_limit_bytes=8 << 20),
+        out_shape=(
+            jax.ShapeDtypeStruct((CHAINS, 2, 2, HALF, W), f32),
+            jax.ShapeDtypeStruct((CHAINS, 2, P_SIZE), f32),
+        ),
+        in_specs=[far, far],
+        out_specs=(far, far),
+        scratch_shapes=[
+            pltpu.VMEM((4, DEVICES * 8, HALF), f32),
+            pltpu.VMEM((CHAINS, 2, 2, HALF, W), f32),
+            pltpu.VMEM((CHAINS, 2, P_SIZE), f32),
+            dma((4,)),
+            dma((4,)),
+            dma((2,)),
+        ],
+        compiler_params=pltpu.CompilerParams(vmem_limit_bytes=VMEM_ALL),
         name="unblock",
-    )(back)
-    return field_out, particles
+    )(back, ended)
+    return field_out.reshape(CHAINS, 2, W, W), particles
 
 
 def solution(mesh):

time: 101 us -> 95 us (0.941)
  the two profiles are of different devices: /device:TPU:3 before, /device:TPU:35 now
where the time goes in v2:
time: 95 us; the launch traced here: 94.2 us
  Pallas kernels  93.4 us (98%)
    pallas_call x1, Pallas kernels, on_device(): pl.pallas_call(whole_kernel, out_shape=(jax.ShapeDtypeStruct((4, DEVICES...  90.5 us
    pallas_call x1, Pallas kernels, on_device(): pl.pallas_call(unblock_kernel, out_shape=(jax.ShapeDtypeStruct((CHAINS, 2...  2.88 us

profile of v2, /device:TPU:35, one launch (start us, length us, event | category | flops | bytes accessed | tf_op | source)
XLA Modules:
  0.0 94.2 jit_solution(2528310831605228538)
XLA Ops:
  0.6 90.5 %pass.1 = (f32[4,1024,128]{2,1,0:T(8,128)}, f32[4,2,1024]{2,1,0:T(2,128)}) custom-call(s32[4]{0:T(128)} %plan.1, f32[4,2,256,256]{3,2,1,0:T(8,128)} %field_in.1, f32[4,1024]{1,0:T(4,128)} %phases_in.1, f32[4,1024]{1,0:T(4,128)} %energy_in.1, s32[4,2,1024]{2,1,0:T(2,128)} %cells_in.1, f32[4,2,1024]{2,1,0:T(2,128)} %shifts_in.1, f32[2,512]{1,0:T(2,128)} %bragg_in.1, ...), custom_call_target="tpu_custom_call" | custom-call | tf_op jit(solution)/shard_map/pass/pallas_call | solution.py:472
  91.1 2.9 %unblock.1 = (f32[4,2,2,128,256]{4,3,2,1,0:T(8,128)}, f32[4,2,1024]{2,1,0:T(2,128)}) custom-call(f32[4,1024,128]{2,1,0:T(8,128)} %get-tuple-element.6.blocks, f32[4,2,1024]{2,1,0:T(2,128)} %get-tuple-element.7.ended), custom_call_target="tpu_custom_call" | custom-call | tf_op jit(solution)/shard_map/unblock/pallas_call | solution.py:529

commit v3 on v2

--- a/solution.py
+++ b/solution.py
@@ -146,8 +146,6 @@
     for copy in tables:
         copy.start()
     barrier = pltpu.get_barrier_semaphore()
-    for there in others:
-        pl.semaphore_signal(barrier, inc=1, device_id=there, device_id_type=MESH)
     grid[...] = lax.broadcasted_iota(jnp.int32, (W, W), 0).astype(f32).astype(bf16)
 
     def build(r, carry):
@@ -159,32 +157,35 @@
         copy.wait()
     gcells[0:CHAINS] = cells[...]
     gshifts[0:CHAINS] = shifts[...]
-    lax.fori_loop(0, CHAINS, build, 0)
+    for r in range(2):
+        build(r, 0)
     load.wait()
     for copy in tables:
         copy.wait()
 
-    def advance(u, base, theta):
+    def deposit(u, base, theta):
         sine, cosine = sincos(theta)
         for k in range(2):
             r = base + k + met[u]
-            c, s = cosine[k : k + 1].astype(bf16), -sine[k : k + 1].astype(bf16)
+            c, s = (GAIN * cosine[k : k + 1]).astype(bf16), (-GAIN * sine[k : k + 1]).astype(bf16)
             for row in range(0, W, 64):
                 weights = tx[r, row : row + 64, :]
                 dep[k, row : row + 64, :] = weights * c
                 dep[k, W + row : W + row + 64, :] = weights * s
-            cur[k] = lax.dot_general(dep[k], ty[r], (((1,), (1,)), ((), ())), preferred_element_type=f32)
+            cur[base + k] = lax.dot_general(dep[k], ty[r], (((1,), (1,)), ((), ())), preferred_element_type=f32)
+        return sine, cosine
+
+    def diffract(u, base):
         for k in range(2):
             chain = base + k
             at = me * CHAINS + chain
-            keep = 1.0
-            if u:
-                keep = jnp.where((at + met[u] >= NS) & (at + met[u - 1] < NS), 0.0, 1.0)
+            keep = jnp.where((at + met[u] >= NS) & (at + met[u - 1] < NS), 0.0, 1.0) if u else None
+            kept = (lambda value, keep=keep: value * keep) if u else (lambda value: value)
             for c in range(2):
                 for row in range(0, HALF, 32):
-                    top = field[chain, c, row : row + 32, :] * keep + GAIN * cur[k, c * W + row : c * W + row + 32, :]
+                    top = kept(field[chain, c, row : row + 32, :]) + cur[chain, c * W + row : c * W + row + 32, :]
                     low = row + HALF
-                    bottom = field[chain, c, low : low + 32, :] * keep + GAIN * cur[k, c * W + low : c * W + low + 32, :]
+                    bottom = kept(field[chain, c, low : low + 32, :]) + cur[chain, c * W + low : c * W + low + 32, :]
                     for sx, v in enumerate((top + bottom, top - bottom)):
                         a, b = v[:, :HALF], v[:, HALF:]
                         rows = slice(sx * HALF + row, sx * HALF + row + 32)
@@ -219,7 +220,6 @@
                         else:
                             gone = (at + met[STEPS] >= NS) & (at + met[STEPS - 1] < NS)
                             sent[base + hy, pl.ds(hx * 4 + c * 2 + k, HALF, stride=8), :] = g * jnp.where(gone, 0.0, 1.0)
-        return sine, cosine
 
     def push(u, base, theta, eta, sine, cosine):
         sampled = []
@@ -228,8 +228,12 @@
             pieces = []
             for q in range(0, P_SIZE, 256):
                 picked = jnp.dot(rounded[base + k], ty[r, :, q : q + 256], preferred_element_type=f32)
-                weights = tx[r, :, q : q + 256].astype(f32)
-                pieces.append([jnp.sum(picked[c * W : c * W + W] * weights, axis=0, keepdims=True) for c in range(2)])
+                sums = [jnp.zeros((16, 256), f32) for c in range(2)]
+                for row in range(0, W, 16):
+                    weights = tx[r, row : row + 16, q : q + 256].astype(f32)
+                    for c in range(2):
+                        sums[c] = sums[c] + picked[c * W + row : c * W + row + 16] * weights
+                pieces.append([jnp.sum(total, axis=0, keepdims=True) for total in sums])
             sampled.append([jnp.concatenate([piece[c] for piece in pieces], axis=1) for c in range(2)])
         first = jnp.concatenate([sampled[0][0], sampled[1][0]], axis=0)
         second = jnp.concatenate([sampled[0][1], sampled[1][1]], axis=0)
@@ -275,22 +279,33 @@
     moving = []
     for u in range(STEPS - 1):
         theta, eta = front(u)
-        push(u, 0, theta, eta, *advance(u, 0, theta))
+        turn = deposit(u, 0, theta)
+        if u == 0:
+            for there in others:
+                pl.semaphore_signal(barrier, inc=1, device_id=there, device_id_type=MESH)
+        if u == 0:
+            for r in range(2, CHAINS):
+                build(r, 0)
+        if u == 1:
+            for copy in geometry:
+                copy.wait()
+            for r in range(CHAINS, REACH):
+                build(r, 0)
+        diffract(u, 0)
         if u == 0:
             pl.semaphore_wait(barrier, DEVICES - 1)
             for copy in geometry:
                 copy.start()
         for copy in moving:
             copy.wait()
-        if u == 1:
-            for copy in geometry:
-                copy.wait()
-            lax.fori_loop(CHAINS, REACH, build, 0)
+        rear_theta, rear_eta = rear(u)
+        push(u, 0, theta, eta, *turn)
+        rear_turn = deposit(u, 2, rear_theta)
         moving = exchange(u)
         for copy in moving:
             copy.start()
-        theta, eta = rear(u)
-        push(u, 2, theta, eta, *advance(u, 2, theta))
+        diffract(u, 2)
+        push(u, 2, rear_theta, rear_eta, *rear_turn)
     last = STEPS - 1
     def spread(src, dst, first, count, ss, rs):
         parts = pl.ds(first, count)
@@ -305,12 +320,14 @@
         pltpu.make_async_copy(view, view, sem).wait()
 
     ahead = front(last)
-    ahead_turn = advance(last, 0, ahead[0])
+    ahead_turn = deposit(last, 0, ahead[0])
+    diffract(last, 0)
     spread(sent, got, 0, 2, s1.at[0], r1.at[0])
     for copy in moving:
         copy.wait()
     behind = rear(last)
-    behind_turn = advance(last, 2, behind[0])
+    behind_turn = deposit(last, 2, behind[0])
+    diffract(last, 2)
     spread(sent, got, 2, 1, s1.at[1], r1.at[1])
     spread(sent, got, 3, 1, s1.at[2], r1.at[2])
     mine = pl.ds(pl.multiple_of(me * 8, 8), 8)
@@ -492,7 +509,7 @@
             pltpu.VMEM((STEPS, 2, CHAINS, P_SIZE), f32),
             pltpu.VMEM((STEPS, 2, 2, P_SIZE), f32),
             pltpu.VMEM((2, 2 * W, P_SIZE), bf16),
-            pltpu.VMEM((2, 2 * W, W), f32),
+            pltpu.VMEM((CHAINS, 2 * W, W), f32),
             pltpu.VMEM((2, 3 * W, W), bf16),
             pltpu.VMEM((2, W, 3 * W), bf16),
             pltpu.VMEM((2, 2, W, 3 * W), bf16),

time: 95 us -> 98.3 us (1.035)
  Pallas kernels: 93.4 us -> 97.3 us
    pallas_call x1, Pallas kernels: 90.5 us -> 94.4 us  [on_device(): pl.pallas_call(whole_kernel, out_shape=(jax.ShapeDtypeStruct((4, DEVICES...]
where the time goes in v3:
time: 98.3 us; the launch traced here: 98.1 us
  Pallas kernels  97.3 us (99%)
    pallas_call x1, Pallas kernels, on_device(): pl.pallas_call(whole_kernel, out_shape=(jax.ShapeDtypeStruct((4, DEVICES...  94.4 us
    pallas_call x1, Pallas kernels, on_device(): pl.pallas_call(unblock_kernel, out_shape=(jax.ShapeDtypeStruct((CHAINS, 2...  2.88 us

profile of v3, /device:TPU:35, one launch (start us, length us, event | category | flops | bytes accessed | tf_op | source)
XLA Modules:
  0.0 98.1 jit_solution(2851236141002068703)
XLA Ops:
  0.6 94.4 %pass.1 = (f32[4,1024,128]{2,1,0:T(8,128)}, f32[4,2,1024]{2,1,0:T(2,128)}) custom-call(s32[4]{0:T(128)} %plan.1, f32[4,2,256,256]{3,2,1,0:T(8,128)} %field_in.1, f32[4,1024]{1,0:T(4,128)} %phases_in.1, f32[4,1024]{1,0:T(4,128)} %energy_in.1, s32[4,2,1024]{2,1,0:T(2,128)} %cells_in.1, f32[4,2,1024]{2,1,0:T(2,128)} %shifts_in.1, f32[2,512]{1,0:T(2,128)} %bragg_in.1, ...), custom_call_target="tpu_custom_call" | custom-call | tf_op jit(solution)/shard_map/pass/pallas_call | solution.py:489
  95.1 2.9 %unblock.1 = (f32[4,2,2,128,256]{4,3,2,1,0:T(8,128)}, f32[4,2,1024]{2,1,0:T(2,128)}) custom-call(f32[4,1024,128]{2,1,0:T(8,128)} %get-tuple-element.6.blocks, f32[4,2,1024]{2,1,0:T(2,128)} %get-tuple-element.7.ended), custom_call_target="tpu_custom_call" | custom-call | tf_op jit(solution)/shard_map/unblock/pallas_call | solution.py:546

commit v4 on v3

--- a/solution.py
+++ b/solution.py
@@ -21,7 +21,7 @@
 GAIN = 0.25 * W * W / P_SIZE
 SPREAD = 20.0
 VMEM_ALL = 67043328
-MESH = pl.DeviceIdType.MESH
+FLAT = pl.DeviceIdType.LOGICAL
 f32, bf16 = jnp.float32, jnp.bfloat16
 
 
@@ -46,8 +46,7 @@
 
 
 def place(n):
-    n = lax.rem(n + 2 * DEVICES, DEVICES)
-    return (n // FINE, lax.rem(n, FINE))
+    return lax.rem(n + 2 * DEVICES, DEVICES)
 
 
 def far_first():
@@ -61,11 +60,13 @@
     coarse, fine = lax.axis_index("coarse"), lax.axis_index("fine")
     x, y = fine // 4, coarse // 2
     z, core = (lax.rem(fine, 4) // 2) * 2 + lax.rem(coarse, 2), lax.rem(fine, 2)
-    out = []
-    for dx, dy, dz, dk in far_first():
-        px, py, pz, pk = lax.rem(x + dx, 4), lax.rem(y + dy, 4), lax.rem(z + dz, 4), lax.rem(core + dk, 2)
-        out.append((py * 2 + lax.rem(pz, 2), px * 4 + (pz // 2) * 2 + pk))
-    return out
+    def turned(v, d):
+        return lax.rem(v + d, 4)
+
+    planes = [[turned(x, dx) * 4 + turned(y, dy) * 2 * FINE for dy in range(4)] for dx in range(4)]
+    depths = [lax.rem(turned(z, dz), 2) * FINE + (turned(z, dz) // 2) * 2 for dz in range(4)]
+    lines = [[depth + lax.rem(core + dk, 2) for dk in range(2)] for depth in depths]
+    return [planes[dx][dy] + lines[dz][dk] for dx, dy, dz, dk in far_first()]
 
 
 def sincos(x):
@@ -146,19 +147,20 @@
     for copy in tables:
         copy.start()
     barrier = pltpu.get_barrier_semaphore()
+    for there in others:
+        pl.semaphore_signal(barrier, inc=1, device_id=there, device_id_type=FLAT)
     grid[...] = lax.broadcasted_iota(jnp.int32, (W, W), 0).astype(f32).astype(bf16)
 
-    def build(r, carry):
-        spline_rows(tx, r, grid, gcells[r, 0:1, :], gshifts[r, 0:1, :])
-        spline_rows(ty, r, grid, gcells[r, 1:2, :], gshifts[r, 1:2, :])
-        return carry
+    def fill_table(r, axis):
+        spline_rows((tx, ty)[axis], r, grid, gcells[r, axis : axis + 1, :], gshifts[r, axis : axis + 1, :])
 
     for copy in small:
         copy.wait()
     gcells[0:CHAINS] = cells[...]
     gshifts[0:CHAINS] = shifts[...]
     for r in range(2):
-        build(r, 0)
+        for axis in range(2):
+            fill_table(r, axis)
     load.wait()
     for copy in tables:
         copy.wait()
@@ -175,7 +177,13 @@
             cur[base + k] = lax.dot_general(dep[k], ty[r], (((1,), (1,)), ((), ())), preferred_element_type=f32)
         return sine, cosine
 
-    def diffract(u, base):
+    def diffract(u, base, slices=()):
+        jobs = [(r, axis) for r in slices for axis in range(2)]
+
+        def work():
+            if jobs:
+                fill_table(*jobs.pop(0))
+
         for k in range(2):
             chain = base + k
             at = me * CHAINS + chain
@@ -196,6 +204,7 @@
                             lhs[k, sy, rows, 2 * W + c * HALF : 2 * W + c * HALF + HALF] = lo
             for sy in range(2):
                 mid = jnp.dot(lhs[k, sy], mright[sy], preferred_element_type=f32)
+                work()
                 for sx in range(2):
                     for c in range(2):
                         hi, lo = split(mid[sx * HALF : sx * HALF + HALF, c * HALF : c * HALF + HALF])
@@ -208,6 +217,7 @@
             at = me * CHAINS + chain
             za = jnp.dot(mleft[0], rhs[k, 0], preferred_element_type=f32)
             zb = jnp.dot(mleft[1], rhs[k, 1], preferred_element_type=f32)
+            work()
             for c in range(2):
                 p, n = za[c * HALF : c * HALF + HALF], zb[c * HALF : c * HALF + HALF]
                 for hx, v in enumerate((p + n, p - n)):
@@ -245,17 +255,17 @@
         return [
             pltpu.make_async_remote_copy(
                 state.at[u, n, pl.ds(0, 2)], arrived.at[u, n], ps.at[u, n], pr.at[u, n],
-                device_id=place(me - 1), device_id_type=MESH)
+                device_id=place(me - 1), device_id_type=FLAT)
             for n in range(2)
         ]
 
     geometry = []
     for n, (src, dst) in enumerate(((cells, gcells), (shifts, gshifts))):
         geometry.append(pltpu.make_async_remote_copy(
-            src, dst.at[pl.ds(4, 4)], gs.at[n], gr.at[n], device_id=place(me - 1), device_id_type=MESH))
+            src, dst.at[pl.ds(4, 4)], gs.at[n], gr.at[n], device_id=place(me - 1), device_id_type=FLAT))
         geometry.append(pltpu.make_async_remote_copy(
             src.at[pl.ds(0, 2)], dst.at[pl.ds(8, 2)], gs.at[n + 2], gr.at[n + 2],
-            device_id=place(me - 2), device_id_type=MESH))
+            device_id=place(me - 2), device_id_type=FLAT))
 
     def front(u):
         if not u:
@@ -280,18 +290,10 @@
     for u in range(STEPS - 1):
         theta, eta = front(u)
         turn = deposit(u, 0, theta)
-        if u == 0:
-            for there in others:
-                pl.semaphore_signal(barrier, inc=1, device_id=there, device_id_type=MESH)
-        if u == 0:
-            for r in range(2, CHAINS):
-                build(r, 0)
         if u == 1:
             for copy in geometry:
                 copy.wait()
-            for r in range(CHAINS, REACH):
-                build(r, 0)
-        diffract(u, 0)
+        diffract(u, 0, ((2, 3), (4, 5), (7,))[u])
         if u == 0:
             pl.semaphore_wait(barrier, DEVICES - 1)
             for copy in geometry:
@@ -304,16 +306,15 @@
         moving = exchange(u)
         for copy in moving:
             copy.start()
-        diffract(u, 2)
+        diffract(u, 2, ((), (6,), (8, 9))[u])
         push(u, 2, rear_theta, rear_eta, *rear_turn)
     last = STEPS - 1
     def spread(src, dst, first, count, ss, rs):
         parts = pl.ds(first, count)
         for there in others:
-            n = there[0] * FINE + there[1]
             pltpu.make_async_remote_copy(
-                src.at[parts, pl.ds(n * 8, 8)], dst.at[parts, pl.ds(me * 8, 8)], ss, rs,
-                device_id=there, device_id_type=MESH).start()
+                src.at[parts, pl.ds(there * 8, 8)], dst.at[parts, pl.ds(me * 8, 8)], ss, rs,
+                device_id=there, device_id_type=FLAT).start()
 
     def settle(ref, count, sem):
         view = ref.at[pl.ds(0, count), pl.ds(0, (DEVICES - 1) * 8)]
@@ -337,7 +338,7 @@
     push(last, 2, *behind, *behind_turn)
     homing = [
         pltpu.make_async_remote_copy(
-            state.at[last], homes.at[n], hs.at[n], hr.at[n], device_id=place(me + n + 1), device_id_type=MESH)
+            state.at[last], homes.at[n], hs.at[n], hr.at[n], device_id=place(me + n + 1), device_id_type=FLAT)
         for n in range(2)
     ]
     for copy in homing:

time: 98.3 us -> 88.4 us (0.90)
  Pallas kernels: 97.3 us -> 87.4 us
    pallas_call x1, Pallas kernels: 94.4 us -> 84.5 us  [on_device(): pl.pallas_call(whole_kernel, out_shape=(jax.ShapeDtypeStruct((4, DEVICES...]
where the time goes in v4:
time: 88.4 us; the launch traced here: 88.2 us
  Pallas kernels  87.4 us (99%)
    pallas_call x1, Pallas kernels, on_device(): pl.pallas_call(whole_kernel, out_shape=(jax.ShapeDtypeStruct((4, DEVICES...  84.5 us
    pallas_call x1, Pallas kernels, on_device(): pl.pallas_call(unblock_kernel, out_shape=(jax.ShapeDtypeStruct((CHAINS, 2...  2.88 us

profile of v4, /device:TPU:35, one launch (start us, length us, event | category | flops | bytes accessed | tf_op | source)
XLA Modules:
  0.0 88.2 jit_solution(3945395389537185963)
XLA Ops:
  0.6 84.5 %pass.1 = (f32[4,1024,128]{2,1,0:T(8,128)}, f32[4,2,1024]{2,1,0:T(2,128)}) custom-call(s32[4]{0:T(128)} %plan.1, f32[4,2,256,256]{3,2,1,0:T(8,128)} %field_in.1, f32[4,1024]{1,0:T(4,128)} %phases_in.1, f32[4,1024]{1,0:T(4,128)} %energy_in.1, s32[4,2,1024]{2,1,0:T(2,128)} %cells_in.1, f32[4,2,1024]{2,1,0:T(2,128)} %shifts_in.1, f32[2,512]{1,0:T(2,128)} %bragg_in.1, ...), custom_call_target="tpu_custom_call" | custom-call | tf_op jit(solution)/shard_map/pass/pallas_call | solution.py:490
  85.1 2.9 %unblock.1 = (f32[4,2,2,128,256]{4,3,2,1,0:T(8,128)}, f32[4,2,1024]{2,1,0:T(2,128)}) custom-call(f32[4,1024,128]{2,1,0:T(8,128)} %get-tuple-element.6.blocks, f32[4,2,1024]{2,1,0:T(2,128)} %get-tuple-element.7.ended), custom_call_target="tpu_custom_call" | custom-call | tf_op jit(solution)/shard_map/unblock/pallas_call | solution.py:547
